TPU v7x, 32 devices: a whole 2x2x4 slice. The times are simulated.
32 devices in a mesh: sec: 8 (over y, x, core), tp: 4 (over z).
Axes of the slice: x: 2, y: 2, z: 4, core: 2. Of those that a mesh axis runs over, the one named last changes fastest.
Arguments:
- queries: bfloat16 [8, 512, 4096], P('sec', 'tp'), may hold values from -5 to 5
- key_rows: bfloat16 [8, 512, 4096], P('sec', 'tp'), may hold values from -5 to 5
- value_rows: bfloat16 [8, 512, 4096], P('sec', 'tp'), may hold values from -6 to 6
- doc_ids: int32 [8, 512], P('sec'), may hold values from 0 to 15, never falling along the last dimension, each value on 1 to 64 neighbouring positions
- rewards: float32 [8, 512], P('sec', 'tp'), may hold values from -12 to 12
- value_head: float32 [4096], replicated, may hold values from -0.375 to 0.375
Outputs:
- attended: bfloat16 [8, 512, 4096], P('sec', 'tp')
- advantages: float32 [8, 512], P('sec', 'tp')
Inputs may be any that keep to these rules, and one draw needn't show every extreme that they name: `doc_ids`: document numbers never fall along a micro-batch, each document spans 1 to 64 tokens, and some document exactly that many.
All inputs are finite; a program needn't handle non-finite values.
Results may differ from a plain program's by a relative error of at most 0.0023.
Values may be sent and summed in bfloat16 or wider, within the bound.
A program may use at most 64 MiB of HBM per device.

v0:
```python
import jax
import jax.numpy as jnp
from jax import lax
from jax.sharding import PartitionSpec as P

HEAD = 128
HEADS = 32


gae_decay = 0.95
epsilon = 1e-05


def shifted(shard, axis, by):
    devices = lax.axis_size(axis)
    pairs = [(i, i + by) for i in range(devices) if 0 <= i + by < devices]
    return lax.ppermute(shard, axis, pairs)


def local(queries, key_rows, value_rows, doc_ids, rewards, value_head):
    count_rows = queries.shape[1]
    start = lax.axis_index("tp") * count_rows
    width = count_rows // 2
    carried = shifted(
        jnp.stack([key_rows[0, count_rows - width :], value_rows[0, count_rows - width :]]), "tp", 1
    )
    query_heads = queries[0].reshape(count_rows, HEADS, HEAD)
    key_heads = jnp.concatenate([carried[0], key_rows[0]], axis=0).reshape(
        width + count_rows, HEADS, HEAD
    )
    value_heads = jnp.concatenate([carried[1], value_rows[0]], axis=0).reshape(
        width + count_rows, HEADS, HEAD
    )
    doc_row = doc_ids[0]
    filler = jnp.full((count_rows,), -1, jnp.int32)
    padded = jnp.concatenate([filler, doc_row, filler[:1]])
    query_doc = lax.dynamic_slice_in_dim(padded, start + count_rows, count_rows)
    key_doc = lax.dynamic_slice_in_dim(padded, start + count_rows - width, width + count_rows)
    next_doc = lax.dynamic_slice_in_dim(padded, start + 2 * count_rows, 1)[0]
    offsets = jnp.arange(count_rows, dtype=jnp.int32)
    query_pos = start + offsets
    key_pos = start - width + jnp.arange(width + count_rows, dtype=jnp.int32)
    allowed = (key_pos[None, :] <= query_pos[:, None]) & (key_doc[None, :] == query_doc[:, None])
    scores = jnp.einsum(
        "qhd,khd->hqk", query_heads, key_heads, preferred_element_type=jnp.float32
    ) * HEAD ** (-0.5)
    scores = jnp.where(allowed[None], scores, jnp.float32(-1e30))
    top = jnp.max(scores, axis=-1, keepdims=True)
    expo = jnp.where(allowed[None], jnp.exp(scores - top), jnp.float32(0.0))
    total = jnp.sum(expo, axis=-1)
    weights = expo.astype(jnp.bfloat16)
    output = jnp.einsum("hqk,khd->qhd", weights, value_heads, preferred_element_type=jnp.float32)
    output = output / jnp.transpose(total)[:, :, None]
    attended_rows = output.astype(jnp.bfloat16).reshape(count_rows, HEADS * HEAD)
    state = jnp.dot(attended_rows.astype(jnp.float32), value_head, precision=lax.Precision.HIGHEST)
    doc_after = jnp.concatenate([query_doc[1:], jnp.full((1,), -2, jnp.int32)])
    linked = query_doc == doc_after
    state_after = jnp.concatenate([state[1:], jnp.zeros((1,), jnp.float32)])
    delta_local = rewards[0] + jnp.where(linked, state_after, jnp.float32(0.0)) - state
    distance = offsets[None, :] - offsets[:, None]
    decay_table = jnp.where(
        (distance >= 0) & (query_doc[None, :] == query_doc[:, None]),
        jnp.power(jnp.float32(gae_decay), distance.astype(jnp.float32)),
        jnp.float32(0.0),
    )
    gae_local = jnp.dot(decay_table, delta_local, precision=lax.Precision.HIGHEST)
    received = shifted(jnp.stack([state[0], gae_local[0]]), "tp", -1)
    joined = query_doc == next_doc
    reach = (count_rows - offsets).astype(jnp.float32)
    correction = (
        jnp.power(jnp.float32(gae_decay), reach - 1.0) * received[0]
        + jnp.power(jnp.float32(gae_decay), reach) * received[1]
    )
    gae = gae_local + jnp.where(joined, correction, jnp.float32(0.0))
    total_sum, square_sum = lax.psum((jnp.sum(gae), jnp.sum(gae * gae)), ("sec", "tp"))
    number = lax.axis_size("sec") * lax.axis_size("tp") * count_rows
    mean = total_sum / number
    spread = square_sum / number - mean * mean
    advantages = (gae - mean) / jnp.sqrt(spread + epsilon)
    return (attended_rows[None], advantages[None])


def solution(mesh):
    return jax.shard_map(
        local,
        mesh=mesh,
        in_specs=(
            P("sec", "tp", None),
            P("sec", "tp", None),
            P("sec", "tp", None),
            P("sec", None),
            P("sec", "tp"),
            P(),
        ),
        out_specs=(P("sec", "tp", None), P("sec", "tp")),
        check_vma=False,
    )
```

profile of v0, /device:TPU:0, one launch (start us, length us, event | category | flops | bytes accessed | tf_op | source)
XLA Modules:
  0.0 90.9 jit_solution(4319487118648748502)
XLA Ops:
  0.7 1.2 %slice.30 = bf16[1,64,4096]{2,1,0:T(8,128)(2,1)S(1)} slice(bf16[1,128,4096]{2,1,0:T(8,128)(2,1)} %param.7), slice={[0:1], [64:128], [0:4096]} | slice | bytes 1048576 | tf_op jit(solution)/shard_map/slice | solution.py:25
  1.9 1.1 %slice.31 = bf16[1,64,4096]{2,1,0:T(8,128)(2,1)S(1)} slice(bf16[1,128,4096]{2,1,0:T(8,128)(2,1)} %param.8), slice={[0:1], [64:128], [0:4096]} | slice | bytes 1048576 | tf_op jit(solution)/shard_map/slice | solution.py:25
  3.0 1.1 %pad_maximum_fusion = bf16[2,64,4096]{2,1,0:T(8,128)(2,1)} fusion(bf16[1,64,4096]{2,1,0:T(8,128)(2,1)S(1)} %slice.31, bf16[1,64,4096]{2,1,0:T(8,128)(2,1)S(1)} %slice.30), kind=kLoop, calls=%fused_computation.19 | loop fusion | flops 524288 | bytes 2097152 | tf_op jit(solution)/shard_map/stack | solution.py:25
  4.1 6.0 %collective-permute-start = (bf16[2,64,4096]{2,1,0:T(8,128)(2,1)}, bf16[2,64,4096]{2,1,0:T(8,128)(2,1)}, u32[]{:S(2)}, u32[]{:S(2)}) collective-permute-start(bf16[2,64,4096]{2,1,0:T(8,128)(2,1)} %pad_maximum_fusion), channel_id=1, source_target_pairs={{0,1},{1,2},{2,3},{4,5},{5,6},{6,7},{8,9},{9,10},{10,11},{12,13},{... | collective-permute-start | bytes 3145736 | tf_op jit(solution)/shard_map/ppermute | solution.py:17
  10.1 0.7 copy.13
  10.7 0.7 copy.10
  11.4 0.1 dynamic_slice.10
  11.6 0.7 copy.15
  12.3 1.4 %copy.20 = bf16[16,8,32,128]{3,2,1,0:T(8,128)(2,1)S(1)} copy(bf16[16,8,32,128]{3,1,2,0:T(8,128)(2,1)} %bitcast.63) | data formatting | bytes 2097152
  13.7 1.3 %copy.12 = bf16[128,32,128]{2,0,1:T(8,128)(2,1)} copy(bf16[128,32,128]{0,2,1:T(8,128)(2,1)S(1)} %bitcast.56) | data formatting | bytes 2097152 | tf_op jit(solution)/shard_map/concatenate | solution.py:31
  15.1 0.6 dynamic_slice.11
  15.7 0.1 compare_and_fusion
  15.8 15.9 %collective-permute-done = bf16[2,64,4096]{2,1,0:T(8,128)(2,1)} collective-permute-done((bf16[2,64,4096]{2,1,0:T(8,128)(2,1)}, bf16[2,64,4096]{2,1,0:T(8,128)(2,1)}, u32[]{:S(2)}, u32[]{:S(2)}) %collective-permute-start) | collective-permute-done | bytes 1048608 | tf_op jit(solution)/shard_map/ppermute | solution.py:17
  31.7 1.3 %slice_bitcast_fusion = (bf16[8,8,32,128]{3,1,2,0:T(8,128)(2,1)S(1)}, bf16[8,8,32,128]{3,1,2,0:T(8,128)(2,1)S(1)}) fusion(bf16[2,64,4096]{2,1,0:T(8,128)(2,1)} %collective-permute-done), kind=kLoop, calls=%fused_computation.21 | loop fusion | bytes 2097152
  33.0 0.1 copy.19
  33.1 0.2 copy.14
  33.3 0.1 copy.18
  33.4 0.2 copy.11
  33.7 0.8 fusion.6
  34.5 1.1 %fusion.43 = (f32[32,128]{1,0:T(8,128)S(1)}, bf16[32,128,192]{1,2,0:T(8,128)(2,1)S(1)}) fusion(f32[32,192,128]{2,1,0:T(8,128)S(1)} %fusion.6, pred[128,192]{0,1:T(8,128)(4,1)S(1)} %compare_and_fusion), kind=kOutput, calls=%fused_computation.58 | output fusion | flops 6291647 | bytes 4759552 | tf_op jit(solution)/shard_map/sub | solution.py:49
  35.6 0.1 copy-done.3
  35.7 0.8 fusion.2
  36.5 0.5 convolution_bitcast_fusion
  37.1 0.3 convolution_bitcast_fusion.1
  37.4 0.2 pad_maximum_fusion.1
  37.5 1.3 %collective-permute-start.1 = (f32[2]{0:T(128)S(1)}, f32[2]{0:T(128)S(1)}, u32[]{:S(2)}, u32[]{:S(2)}) collective-permute-start(f32[2]{0:T(128)S(1)} %pad_maximum_fusion.1), channel_id=1, source_target_pairs={{1,0},{2,1},{3,2},{5,4},{6,5},{7,6},{9,8},{10,9},{11,10},{13,12},{... | collective-permute-start | bytes 32 | tf_op jit(solution)/shard_map/ppermute | solution.py:17
  38.8 1.3 %copy.17 = bf16[1,128,4096]{2,1,0:T(8,128)(2,1)} copy(bf16[1,128,4096]{1,2,0:T(8,128)(2,1)S(1)} %bitcast.59) | data formatting | bytes 2097152
  40.1 3.3 %collective-permute-done.1 = f32[2]{0:T(128)S(1)} collective-permute-done((f32[2]{0:T(128)S(1)}, f32[2]{0:T(128)S(1)}, u32[]{:S(2)}, u32[]{:S(2)}) %collective-permute-start.1) | collective-permute-done | bytes 40 | tf_op jit(solution)/shard_map/ppermute | solution.py:17
  43.4 0.6 fusion.42
  44.0 2.6 %fusion.40 = (f32[]{:T(128)}, f32[]{:T(128)}, f32[128]{0:T(128)S(1)}) fusion(f32[128]{0:T(128)S(1)} %convolution_bitcast_fusion.1, f32[]{:T(128)} %bitcast.15, f32[]{:T(128)} %bitcast.14, s32[]{:T(128)} %bitcast.13, s32[641]{0:T(1024)S(1)} %pad_add_fusion, s32[]{:T(128)S(6)} %select_n.28), kind=kLoop, calls=%fused_computation.56 | loop fusion | flops 1534 | bytes 1560 | tf_op jit(solution)/shard_map/reduce_sum | solution.py:75
  46.7 41.1 %all-reduce = (f32[]{:T(128)}, f32[]{:T(128)}) all-reduce(f32[]{:T(128)} %get-tuple-element.7, f32[]{:T(128)} %get-tuple-element.6), channel_id=1, replica_groups=mesh['sec'=8,'tp'=4] {'sec','tp'}, use_global_device_ids=true, to_apply=%region_5.6 | all-reduce | flops 2 | bytes 16 | tf_op jit(solution)/shard_map/psum | solution.py:75
  90.4 0.5 divide_bitcast_fusion
  (18 shorter events, 0.3 us)
Async XLA Ops:
  0.6 35.9 %copy-start = (f32[4096]{0:T(1024)S(1)}, f32[4096]{0:T(1024)}, u32[]{:S(2)}) copy-start(f32[4096]{0:T(1024)} %param.11) | copy-start | bytes 49156
  0.6 9.4 %copy-start.1 = (bf16[1,128,4096]{2,1,0:T(8,128)(2,1)S(1)}, bf16[1,128,4096]{2,1,0:T(8,128)(2,1)}, u32[]{:S(2)}) copy-start(bf16[1,128,4096]{2,1,0:T(8,128)(2,1)} %param.7) | copy-start | bytes 3145732
  0.7 10.1 %copy-start.2 = (bf16[1,128,4096]{2,1,0:T(8,128)(2,1)S(1)}, bf16[1,128,4096]{2,1,0:T(8,128)(2,1)}, u32[]{:S(2)}) copy-start(bf16[1,128,4096]{2,1,0:T(8,128)(2,1)} %param.8) | copy-start | bytes 3145732
  3.0 8.4 %copy-start.4 = (s32[1,512]{1,0:T(1,128)S(1)}, s32[1,512]{1,0:T(1,128)}, u32[]{:S(2)}) copy-start(s32[1,512]{1,0:T(1,128)} %param.9) | copy-start | bytes 6148
  4.1 27.7 %collective-permute-start = (bf16[2,64,4096]{2,1,0:T(8,128)(2,1)}, bf16[2,64,4096]{2,1,0:T(8,128)(2,1)}, u32[]{:S(2)}, u32[]{:S(2)}) collective-permute-start(bf16[2,64,4096]{2,1,0:T(8,128)(2,1)} %pad_maximum_fusion), channel_id=1, source_target_pairs={{0,1},{1,2},{2,3},{4,5},{5,6},{6,7},{8,9},{9,10},{10,11},{12,13},{... | collective-permute-start | bytes 3145736 | tf_op jit(solution)/shard_map/ppermute | solution.py:17
  34.5 1.2 %copy-start.3 = (bf16[128,32,128]{2,0,1:T(8,128)(2,1)S(1)}, bf16[128,32,128]{2,0,1:T(8,128)(2,1)}, u32[]{:S(2)}) copy-start(bf16[128,32,128]{2,0,1:T(8,128)(2,1)} %copy.12) | copy-start | bytes 3145732
  35.7 1.4 %copy-start.5 = (f32[1,128]{1,0:T(1,128)S(1)}, f32[1,128]{1,0:T(1,128)}, u32[]{:S(2)}) copy-start(f32[1,128]{1,0:T(1,128)} %param.10) | copy-start | bytes 1540
  37.5 5.9 %collective-permute-start.1 = (f32[2]{0:T(128)S(1)}, f32[2]{0:T(128)S(1)}, u32[]{:S(2)}, u32[]{:S(2)}) collective-permute-start(f32[2]{0:T(128)S(1)} %pad_maximum_fusion.1), channel_id=1, source_target_pairs={{1,0},{2,1},{3,2},{5,4},{6,5},{7,6},{9,8},{10,9},{11,10},{13,12},{... | collective-permute-start | bytes 32 | tf_op jit(solution)/shard_map/ppermute | solution.py:17
where the time goes:
time: 91.4 us; the launch traced here: 90.9 us
  blocking collectives  41.1 us (45%)
  waiting for transfers between devices  19.2 us (21%)
  local copies, waits for them, and re-layouts  11.9 us (13%)
  starting transfers between devices  7.27 us (8%)
  other arithmetic  5.64 us (6%)
  between operations  3.42 us (4%)
  matrix products  2.38 us (3%)
    psum x1, blocking collectives, local(): lax.psum((jnp.sum(gae), jnp.sum(gae * gae)), ('sec', 'tp'))  41.1 us
    ppermute x2, waiting for transfers between devices, shifted(): return lax.ppermute(shard, axis, pairs)  19.2 us
    ppermute x2, starting transfers between devices, shifted(): return lax.ppermute(shard, axis, pairs)  7.27 us
    unnamed x19, local copies, waits for them, and re-layouts  5.7 us
    reduce_sum x1, other arithmetic, local(): jnp.sum(gae)  2.65 us
  transfers between devices with their start and end apart: 2, of which 2 were waited for; matrix products, arithmetic and copies ran while one was open for 8% of the time, Pallas kernels for 0%

commit v1 on v0

v1 whole, which is shorter than its diff:
```python
import functools
import math

import jax
import jax.numpy as jnp
from jax import lax
from jax.experimental import pallas as pl
from jax.experimental.pallas import tpu as pltpu
from jax.sharding import PartitionSpec as P

HEAD = 128
GROUP = 8

gae_decay = 0.95
epsilon = 1e-05

MESH = pl.DeviceIdType.MESH
F32 = jnp.float32


def kernel(n_sec, n_tp, q_hbm, k_hbm, v_hbm, doc_ref, rew_ref, head_ref, out_hbm, adv_ref,
           qbuf, kbuf, vbuf, obuf, acc, tp_slot, sec_slot,
           load_sem, store_sem, ksend, krecv, vsend, vrecv,
           tp_send, tp_recv, sec_send, sec_recv):
    rows = qbuf.shape[0]
    feat = qbuf.shape[1]
    half = rows // 2
    width = GROUP * HEAD
    chunks = feat // width
    sec = lax.axis_index("sec")
    tp = lax.axis_index("tp")

    loads = [
        pltpu.make_async_copy(q_hbm.at[0], qbuf, load_sem.at[0]),
        pltpu.make_async_copy(k_hbm.at[0], kbuf.at[pl.ds(half, rows)], load_sem.at[1]),
        pltpu.make_async_copy(v_hbm.at[0], vbuf.at[pl.ds(half, rows)], load_sem.at[2]),
    ]
    for load in loads:
        load.start()

    barrier = pltpu.get_barrier_semaphore()
    for d in range(1, n_tp):
        pl.semaphore_signal(barrier, inc=1, device_id={"tp": lax.rem(tp + d, n_tp)}, device_id_type=MESH)
    for d in range(1, n_sec):
        pl.semaphore_signal(barrier, inc=1, device_id={"sec": lax.rem(sec + d, n_sec)}, device_id_type=MESH)
    pl.semaphore_wait(barrier, n_tp + n_sec - 2)

    def exchange(c):
        cols = pl.ds(c * width, width)
        nxt = {"tp": lax.rem(tp + 1, n_tp)}
        return (
            pltpu.make_async_remote_copy(
                src_ref=k_hbm.at[0, pl.ds(half, half), cols], dst_ref=kbuf.at[pl.ds(0, half), cols],
                send_sem=ksend.at[c], recv_sem=krecv.at[c], device_id=nxt, device_id_type=MESH),
            pltpu.make_async_remote_copy(
                src_ref=v_hbm.at[0, pl.ds(half, half), cols], dst_ref=vbuf.at[pl.ds(0, half), cols],
                send_sem=vsend.at[c], recv_sem=vrecv.at[c], device_id=nxt, device_id_type=MESH),
        )

    @pl.when(tp < n_tp - 1)
    def _():
        for c in range(chunks):
            for copy in exchange(c):
                copy.start()

    @pl.when(tp == 0)
    def _():
        kbuf[pl.ds(0, half), :] = jnp.zeros((half, feat), kbuf.dtype)
        vbuf[pl.ds(0, half), :] = jnp.zeros((half, feat), vbuf.dtype)

    start = pl.multiple_of(tp * rows, rows)
    prev = pl.multiple_of(jnp.maximum(tp - 1, 0) * rows, rows)
    after = pl.multiple_of(jnp.minimum(tp + 1, n_tp - 1) * rows, rows)
    doc_row = doc_ref[0:1, pl.ds(start, rows)].astype(F32)
    doc_prev = doc_ref[0:1, pl.ds(prev, rows)].astype(F32)
    doc_next = doc_ref[0:1, pl.ds(after, rows)].astype(F32)[:, 0:1]
    doc_prev = jnp.where(tp > 0, doc_prev, jnp.float32(-1.0))
    doc_key = jnp.broadcast_to(doc_row, (rows, rows))
    doc_query = doc_key.T
    row_id = lax.broadcasted_iota(jnp.int32, (rows, rows), 0)
    col_id = lax.broadcasted_iota(jnp.int32, (rows, rows), 1)
    same = (col_id <= row_id) & (doc_key == doc_query)
    decay_log = math.log(gae_decay)
    table = jnp.where(same, jnp.exp((row_id - col_id).astype(F32) * decay_log), F32(0.0))
    lane = lax.broadcasted_iota(jnp.int32, (half, rows), 1)
    line = lax.broadcasted_iota(jnp.int32, (half, rows), 0)
    key_lo = jnp.broadcast_to(
        jnp.where(lane[0:1] < half, pltpu.roll(doc_prev, half, 1), pltpu.roll(doc_row, half, 1)), (half, rows))
    allowed_lo = (lane - half <= line) & (key_lo == doc_query[0:half])
    allowed_hi = (lane <= line + half) & (doc_key[half:] == doc_query[half:])

    scale = HEAD ** (-0.5)

    def attend(c, first, key_first, allowed):
        total_state = jnp.zeros((half, HEAD), F32)
        spans = [pl.ds(pl.multiple_of(c * width + g * HEAD, HEAD), HEAD) for g in range(GROUP)]
        expos = []
        for g in range(GROUP):
            raw = lax.dot_general(
                qbuf[pl.ds(first, half), spans[g]], kbuf[pl.ds(key_first, rows), spans[g]],
                (((1,), (1,)), ((), ())), preferred_element_type=F32)
            expos.append(jnp.where(allowed, raw * scale, F32(-1e30)))
        for g in range(GROUP):
            top = jnp.max(expos[g], axis=-1, keepdims=True)
            expo = jnp.exp(expos[g] - top)
            total = jnp.sum(expo, axis=-1, keepdims=True)
            summed = jnp.dot(expo.astype(jnp.bfloat16), vbuf[pl.ds(key_first, rows), spans[g]],
                             preferred_element_type=F32)
            result = (summed / total).astype(jnp.bfloat16)
            obuf[pl.ds(first, half), spans[g]] = result
            total_state = total_state + result.astype(F32) * head_ref[0:1, spans[g]]
        return total_state

    for load in loads:
        load.wait()

    acc_hi = lax.fori_loop(
        0, chunks, lambda c, held: held + attend(c, half, half, allowed_hi), jnp.zeros((half, HEAD), F32))
    acc[pl.ds(half, half), :] = acc_hi
    store_hi = pltpu.make_async_copy(
        obuf.at[pl.ds(half, half)], out_hbm.at[0, pl.ds(half, half)], store_sem.at[0])
    store_hi.start()

    acc_lo = jnp.zeros((half, HEAD), F32)
    stores = [store_hi]
    for c in range(chunks):
        @pl.when(tp > 0)
        def _():
            for copy in exchange(c):
                copy.wait_recv()
        acc_lo = acc_lo + attend(c, 0, 0, allowed_lo)
    store_lo = pltpu.make_async_copy(
        obuf.at[pl.ds(0, half)], out_hbm.at[0, pl.ds(0, half)], store_sem.at[1])
    store_lo.start()
    stores.append(store_lo)
    acc[pl.ds(0, half), :] = acc_lo

    state = jnp.sum(acc[...].T, axis=0, keepdims=True)
    spot = lax.broadcasted_iota(jnp.int32, (1, rows), 1)
    linked = (pltpu.roll(doc_row, rows - 1, 1) == doc_row) & (spot < rows - 1)
    delta = rew_ref[...] + jnp.where(linked, pltpu.roll(state, rows - 1, 1), F32(0.0)) - state
    gae_local = jnp.sum(table * jnp.broadcast_to(delta, (rows, rows)).T, axis=0, keepdims=True)
    joined = (doc_row == doc_next) & (tp < n_tp - 1)
    coef = jnp.where(joined, jnp.exp((rows - 1 - spot).astype(F32) * decay_log), F32(0.0))
    carry = state[:, 0:1] + gae_decay * gae_local[:, 0:1]

    def summed(x):
        return jnp.broadcast_to(jnp.sum(x, axis=1, keepdims=True), (1, rows))

    rows_out = [summed(gae_local), summed(gae_local * gae_local), summed(coef),
                summed(coef * gae_local), summed(coef * coef), jnp.broadcast_to(carry, (1, rows))]
    for i, value in enumerate(rows_out):
        tp_slot[tp, pl.ds(i, 1), :] = value

    def tp_copy(d):
        return pltpu.make_async_remote_copy(
            src_ref=tp_slot.at[tp], dst_ref=tp_slot.at[tp], send_sem=tp_send.at[d], recv_sem=tp_recv.at[tp],
            device_id={"tp": lax.rem(tp + d, n_tp)}, device_id_type=MESH)

    def tp_wait(peer):
        return pltpu.make_async_remote_copy(
            src_ref=tp_slot.at[peer], dst_ref=tp_slot.at[peer], send_sem=tp_send.at[0], recv_sem=tp_recv.at[peer],
            device_id={"tp": peer}, device_id_type=MESH)

    for d in range(1, n_tp):
        tp_copy(d).start()
    for d in range(1, n_tp):
        tp_wait(lax.rem(tp + d, n_tp)).wait_recv()

    mean_part = jnp.zeros((1, rows), F32)
    square_part = jnp.zeros((1, rows), F32)
    mine = jnp.zeros((1, rows), F32)
    for t in range(n_tp):
        part = tp_slot[t]
        arrived = tp_slot[t + 1][5:6] if t + 1 < n_tp else jnp.zeros((1, rows), F32)
        mean_part = mean_part + part[0:1] + part[2:3] * arrived
        square_part = square_part + part[1:2] + 2.0 * part[3:4] * arrived + part[4:5] * arrived * arrived
        mine = jnp.where(tp == t, arrived, mine)
    gae = gae_local + coef * mine

    sec_slot[sec, pl.ds(0, 1), :] = mean_part
    sec_slot[sec, pl.ds(1, 1), :] = square_part

    def sec_copy(d):
        return pltpu.make_async_remote_copy(
            src_ref=sec_slot.at[sec], dst_ref=sec_slot.at[sec], send_sem=sec_send.at[d], recv_sem=sec_recv.at[sec],
            device_id={"sec": lax.rem(sec + d, n_sec)}, device_id_type=MESH)

    def sec_wait(peer):
        return pltpu.make_async_remote_copy(
            src_ref=sec_slot.at[peer], dst_ref=sec_slot.at[peer], send_sem=sec_send.at[0],
            recv_sem=sec_recv.at[peer], device_id={"sec": peer}, device_id_type=MESH)

    for d in range(1, n_sec):
        sec_copy(d).start()
    for d in range(1, n_sec):
        sec_wait(lax.rem(sec + d, n_sec)).wait_recv()

    total_sum = jnp.zeros((1, rows), F32)
    square_sum = jnp.zeros((1, rows), F32)
    for s in range(n_sec):
        part = sec_slot[s]
        total_sum = total_sum + part[0:1]
        square_sum = square_sum + part[1:2]
    number = n_sec * n_tp * rows
    mean = total_sum / number
    spread = square_sum / number - mean * mean
    adv_ref[...] = (gae - mean) / jnp.sqrt(spread + epsilon)

    for store in stores:
        store.wait()
    for d in range(1, n_tp):
        tp_copy(d).wait_send()
    for d in range(1, n_sec):
        sec_copy(d).wait_send()

    @pl.when(tp < n_tp - 1)
    def _():
        for c in range(chunks):
            for copy in exchange(c):
                copy.wait_send()


def local(n_sec, n_tp, queries, key_rows, value_rows, doc_ids, rewards, value_head):
    rows, feat = queries.shape[1:]
    half = rows // 2
    chunks = feat // (GROUP * HEAD)
    any_spec = pl.BlockSpec(memory_space=pl.ANY)
    vmem_spec = pl.BlockSpec(memory_space=pltpu.VMEM)
    dma = pltpu.SemaphoreType.DMA
    bf16 = jnp.bfloat16
    return pl.pallas_call(
        functools.partial(kernel, n_sec, n_tp),
        out_shape=(jax.ShapeDtypeStruct((1, rows, feat), bf16), jax.ShapeDtypeStruct((1, rows), F32)),
        in_specs=[any_spec, any_spec, any_spec, vmem_spec, vmem_spec, vmem_spec],
        out_specs=(any_spec, vmem_spec),
        scratch_shapes=[
            pltpu.VMEM((rows, feat), bf16),
            pltpu.VMEM((rows + half, feat), bf16),
            pltpu.VMEM((rows + half, feat), bf16),
            pltpu.VMEM((rows, feat), bf16),
            pltpu.VMEM((rows, HEAD), F32),
            pltpu.VMEM((n_tp, 8, rows), F32),
            pltpu.VMEM((n_sec, 8, rows), F32),
            dma((3,)), dma((2,)),
            dma((chunks,)), dma((chunks,)), dma((chunks,)), dma((chunks,)),
            dma((n_tp,)), dma((n_tp,)), dma((n_sec,)), dma((n_sec,)),
        ],
        compiler_params=pltpu.CompilerParams(collective_id=0, has_side_effects=True),
    )(queries, key_rows, value_rows, doc_ids, rewards, value_head.reshape(1, feat))


def solution(mesh):
    return jax.shard_map(
        functools.partial(local, mesh.shape["sec"], mesh.shape["tp"]),
        mesh=mesh,
        in_specs=(
            P("sec", "tp", None),
            P("sec", "tp", None),
            P("sec", "tp", None),
            P("sec", None),
            P("sec", "tp"),
            P(),
        ),
        out_specs=(P("sec", "tp", None), P("sec", "tp")),
        check_vma=False,
    )
```

time: 91.4 us -> 42.3 us (0.46)
  blocking collectives: 41.1 us -> 0 us
  Pallas kernels: 0 us -> 38.6 us
  waiting for transfers between devices: 19.2 us -> 0 us
  local copies, waits for them, and re-layouts: 11.9 us -> 2.8 us
  starting transfers between devices: 7.27 us -> 0 us
  other arithmetic: 5.64 us -> 0 us
  between operations: 3.42 us -> 0.65 us
  matrix products: 2.38 us -> 0 us
    psum x1 -> x0, blocking collectives: 41.1 us -> none  [local(): lax.psum((jnp.sum(gae), jnp.sum(gae * gae)), ('sec', 'tp'))]
    pallas_call x0 -> x1, Pallas kernels: none -> 38.6 us  [local(): pl.pallas_call(functools.partial(kernel, n_sec, n_tp), out_shape=(jax.Sha...]
    ppermute x2 -> x0, waiting for transfers between devices: 19.2 us -> none  [shifted(): return lax.ppermute(shard, axis, pairs)]
    ppermute x2 -> x0, starting transfers between devices: 7.27 us -> none  [shifted(): return lax.ppermute(shard, axis, pairs)]
    slice x5 -> x0, local copies, waits for them, and re-layouts: 3.06 us -> none  [the longest x1 1.22 us: local(): key_rows[0, count_rows - width:]]
    unnamed x19 -> x4, local copies, waits for them, and re-layouts: 5.7 us -> 2.8 us
    reduce_sum x1 -> x0, other arithmetic: 2.65 us -> none  [local(): jnp.sum(gae)]
    concatenate x4 -> x0, local copies, waits for them, and re-layouts: 2.38 us -> none  [the longest x2 1.52 us: local(): jnp.concatenate([carried[1], value_rows[0]], axis=0)]
  transfers between devices with their start and end apart: 2 -> 0, of which waited for: 2 -> 0; matrix products, arithmetic and copies ran while one was open for 8% -> 0% of each run, Pallas kernels for 0% -> 0%
where the time goes in v1:
time: 42.3 us; the launch traced here: 42 us
  Pallas kernels  38.6 us (91%)
  local copies, waits for them, and re-layouts  2.8 us (7%)
  between operations  0.65 us (2%)
    pallas_call x1, Pallas kernels, local(): pl.pallas_call(functools.partial(kernel, n_sec, n_tp), out_shape=(jax.Sha...  38.6 us
    unnamed x4, local copies, waits for them, and re-layouts  2.8 us

profile of v1, /device:TPU:0, one launch (start us, length us, event | category | flops | bytes accessed | tf_op | source)
XLA Modules:
  0.0 42.0 jit_solution(18110844541096053354)
XLA Ops:
  0.6 38.6 %shard_map.77 = (bf16[1,128,4096]{2,1,0:T(8,128)(2,1)}, f32[1,128]{1,0:T(1,128)}) custom-call(bf16[1,128,4096]{2,1,0:T(8,128)(2,1)} %q_hbm.1, bf16[1,128,4096]{2,1,0:T(8,128)(2,1)} %k_hbm.1, bf16[1,128,4096]{2,1,0:T(8,128)(2,1)} %v_hbm.1, s32[1,512]{1,0:T(1,128)} %doc_ref.1, f32[1,128]{1,0:T(1,128)} %rew_ref.1, f32[1,4096]{1,0:T(1,128)} %bitcast.1), custom_call_target="tpu_custom_call" | custom-call | tf_op jit(solution)/shard_map/pallas_call | solution.py:232
  39.2 0.0 copy-start
  39.2 2.3 %copy.10 = bf16[1,128,4096]{2,1,0:T(8,128)(2,1)} copy(bf16[1,128,4096]{2,1,0:T(8,128)(2,1)} %get-tuple-element.4) | data formatting | bytes 2097152
  41.5 0.0 copy-done
  41.5 0.5 %copy.11 = f32[1,128]{1,0:T(1,128)} copy(f32[1,128]{1,0:T(1,128)S(1)} %copy-done) | data formatting | bytes 1024
Async XLA Ops:
  39.2 2.3 %copy-start = (f32[1,128]{1,0:T(1,128)S(1)}, f32[1,128]{1,0:T(1,128)}, u32[]{:S(2)}) copy-start(f32[1,128]{1,0:T(1,128)} %get-tuple-element.5) | copy-start | bytes 1540

commit v2 on v1

--- a/solution.py
+++ b/solution.py
@@ -19,12 +19,13 @@
 
 
 def kernel(n_sec, n_tp, q_hbm, k_hbm, v_hbm, doc_ref, rew_ref, head_ref, out_hbm, adv_ref,
-           qbuf, kbuf, vbuf, obuf, acc, tp_slot, sec_slot,
-           load_sem, store_sem, ksend, krecv, vsend, vrecv,
+           qbuf, kbuf, vbuf, obuf, q_in, mixed, lse_out, lse_in, acc, tp_slot, sec_slot,
+           load_sem, store_sem, qsend, qrecv, ksend, krecv, vsend, vrecv, lsend, lrecv,
            tp_send, tp_recv, sec_send, sec_recv):
     rows = qbuf.shape[0]
     feat = qbuf.shape[1]
     half = rows // 2
+    part = half // 2
     width = GROUP * HEAD
     chunks = feat // width
     sec = lax.axis_index("sec")
@@ -32,8 +33,8 @@
 
     loads = [
         pltpu.make_async_copy(q_hbm.at[0], qbuf, load_sem.at[0]),
-        pltpu.make_async_copy(k_hbm.at[0], kbuf.at[pl.ds(half, rows)], load_sem.at[1]),
-        pltpu.make_async_copy(v_hbm.at[0], vbuf.at[pl.ds(half, rows)], load_sem.at[2]),
+        pltpu.make_async_copy(k_hbm.at[0], kbuf.at[pl.ds(part, rows)], load_sem.at[1]),
+        pltpu.make_async_copy(v_hbm.at[0], vbuf.at[pl.ds(part, rows)], load_sem.at[2]),
     ]
     for load in loads:
         load.start()
@@ -45,28 +46,52 @@
         pl.semaphore_signal(barrier, inc=1, device_id={"sec": lax.rem(sec + d, n_sec)}, device_id_type=MESH)
     pl.semaphore_wait(barrier, n_tp + n_sec - 2)
 
-    def exchange(c):
-        cols = pl.ds(c * width, width)
-        nxt = {"tp": lax.rem(tp + 1, n_tp)}
-        return (
-            pltpu.make_async_remote_copy(
-                src_ref=k_hbm.at[0, pl.ds(half, half), cols], dst_ref=kbuf.at[pl.ds(0, half), cols],
-                send_sem=ksend.at[c], recv_sem=krecv.at[c], device_id=nxt, device_id_type=MESH),
-            pltpu.make_async_remote_copy(
-                src_ref=v_hbm.at[0, pl.ds(half, half), cols], dst_ref=vbuf.at[pl.ds(0, half), cols],
-                send_sem=vsend.at[c], recv_sem=vrecv.at[c], device_id=nxt, device_id_type=MESH),
-        )
-
-    @pl.when(tp < n_tp - 1)
+    following = {"tp": lax.rem(tp + 1, n_tp)}
+    preceding = {"tp": lax.rem(tp + n_tp - 1, n_tp)}
+
+    def columns(c):
+        return pl.ds(pl.multiple_of(c * width, width), width)
+
+    def send_queries(c):
+        return pltpu.make_async_remote_copy(
+            src_ref=q_hbm.at[0, pl.ds(0, part), columns(c)], dst_ref=q_in.at[:, columns(c)],
+            send_sem=qsend.at[c], recv_sem=qrecv.at[c], device_id=preceding, device_id_type=MESH)
+
+    def send_keys(c):
+        return pltpu.make_async_remote_copy(
+            src_ref=k_hbm.at[0, pl.ds(rows - part, part), columns(c)], dst_ref=kbuf.at[pl.ds(0, part), columns(c)],
+            send_sem=ksend.at[c], recv_sem=krecv.at[c], device_id=following, device_id_type=MESH)
+
+    def send_mixed(c):
+        return pltpu.make_async_remote_copy(
+            src_ref=mixed.at[:, columns(c)], dst_ref=vbuf.at[pl.ds(0, part), columns(c)],
+            send_sem=vsend.at[c], recv_sem=vrecv.at[c], device_id=following, device_id_type=MESH)
+
+    def send_lse():
+        return pltpu.make_async_remote_copy(
+            src_ref=lse_out, dst_ref=lse_in, send_sem=lsend, recv_sem=lrecv,
+            device_id=following, device_id_type=MESH)
+
+    sends_on = tp < n_tp - 1
+    receives = tp > 0
+
+    @pl.when(receives)
     def _():
         for c in range(chunks):
-            for copy in exchange(c):
-                copy.start()
+            send_queries(c).start()
+
+    @pl.when(sends_on)
+    def _():
+        for c in range(chunks):
+            send_keys(c).start()
 
     @pl.when(tp == 0)
     def _():
-        kbuf[pl.ds(0, half), :] = jnp.zeros((half, feat), kbuf.dtype)
-        vbuf[pl.ds(0, half), :] = jnp.zeros((half, feat), vbuf.dtype)
+        kbuf[pl.ds(0, part), :] = jnp.zeros((part, feat), kbuf.dtype)
+        vbuf[pl.ds(0, part), :] = jnp.zeros((part, feat), vbuf.dtype)
+        lse_in[...] = jnp.zeros(lse_in.shape, F32)
+
+    lse_out[...] = jnp.zeros(lse_out.shape, F32)
 
     start = pl.multiple_of(tp * rows, rows)
     prev = pl.multiple_of(jnp.maximum(tp - 1, 0) * rows, rows)
@@ -82,58 +107,118 @@
     same = (col_id <= row_id) & (doc_key == doc_query)
     decay_log = math.log(gae_decay)
     table = jnp.where(same, jnp.exp((row_id - col_id).astype(F32) * decay_log), F32(0.0))
+    before = jnp.sum(jnp.where(doc_prev == doc_row[:, 0:1], F32(1.0), F32(0.0)), axis=1, keepdims=True)
+    before_next = jnp.sum(jnp.where(doc_row == doc_next, F32(1.0), F32(0.0)), axis=1, keepdims=True)
+    given = before > part
+    giving = before_next > part
+    given_rows = given & (doc_query[0:part, 0:1] == doc_prev[:, rows - 1 : rows])
+    doc_keys_prev = jnp.where(given, F32(-1.0), doc_prev)
     lane = lax.broadcasted_iota(jnp.int32, (half, rows), 1)
     line = lax.broadcasted_iota(jnp.int32, (half, rows), 0)
     key_lo = jnp.broadcast_to(
-        jnp.where(lane[0:1] < half, pltpu.roll(doc_prev, half, 1), pltpu.roll(doc_row, half, 1)), (half, rows))
-    allowed_lo = (lane - half <= line) & (key_lo == doc_query[0:half])
+        jnp.where(lane[0:1] < part, pltpu.roll(doc_keys_prev, part, 1), pltpu.roll(doc_row, part, 1)), (half, rows))
+    allowed_lo = (lane - part <= line) & (key_lo == doc_query[0:half])
     allowed_hi = (lane <= line + half) & (doc_key[half:] == doc_query[half:])
+    allowed_next = jnp.broadcast_to(doc_row == doc_next, (part, rows)) & (lane[0:part] >= half)
+    giving_all = jnp.broadcast_to(giving, (part, HEAD))
+    head_lane = lax.broadcasted_iota(jnp.int32, (part, HEAD), 1)
 
     scale = HEAD ** (-0.5)
 
-    def attend(c, first, key_first, allowed):
+    def spans_of(c):
+        return [pl.ds(pl.multiple_of(c * width + g * HEAD, HEAD), HEAD) for g in range(GROUP)]
+
+    def scores(query, key, allowed):
+        raw = lax.dot_general(query, key, (((1,), (1,)), ((), ())), preferred_element_type=F32)
+        return jnp.where(allowed, raw * scale, F32(-1e30))
+
+    def attend_hi(c):
+        spans = spans_of(c)
         total_state = jnp.zeros((half, HEAD), F32)
-        spans = [pl.ds(pl.multiple_of(c * width + g * HEAD, HEAD), HEAD) for g in range(GROUP)]
-        expos = []
-        for g in range(GROUP):
-            raw = lax.dot_general(
-                qbuf[pl.ds(first, half), spans[g]], kbuf[pl.ds(key_first, rows), spans[g]],
-                (((1,), (1,)), ((), ())), preferred_element_type=F32)
-            expos.append(jnp.where(allowed, raw * scale, F32(-1e30)))
-        for g in range(GROUP):
-            top = jnp.max(expos[g], axis=-1, keepdims=True)
-            expo = jnp.exp(expos[g] - top)
+        found = [scores(qbuf[pl.ds(half, half), s], kbuf[pl.ds(part, rows), s], allowed_hi) for s in spans]
+        for g, s in enumerate(spans):
+            top = jnp.max(found[g], axis=-1, keepdims=True)
+            expo = jnp.exp(found[g] - top)
             total = jnp.sum(expo, axis=-1, keepdims=True)
-            summed = jnp.dot(expo.astype(jnp.bfloat16), vbuf[pl.ds(key_first, rows), spans[g]],
-                             preferred_element_type=F32)
-            result = (summed / total).astype(jnp.bfloat16)
-            obuf[pl.ds(first, half), spans[g]] = result
-            total_state = total_state + result.astype(F32) * head_ref[0:1, spans[g]]
+            added = jnp.dot(expo.astype(jnp.bfloat16), vbuf[pl.ds(part, rows), s], preferred_element_type=F32)
+            result = (added / total).astype(jnp.bfloat16)
+            obuf[pl.ds(half, half), s] = result
+            total_state = total_state + result.astype(F32) * head_ref[0:1, s]
+        return total_state
+
+    def attend_next(c):
+        spans = spans_of(c)
+        found = [scores(q_in[:, s], kbuf[pl.ds(part, rows), s], allowed_next) for s in spans]
+        sums = lse_out[...]
+        for g, s in enumerate(spans):
+            top = jnp.max(found[g], axis=-1, keepdims=True)
+            expo = jnp.exp(found[g] - top)
+            total = jnp.sum(expo, axis=-1, keepdims=True)
+            added = jnp.dot(expo.astype(jnp.bfloat16), vbuf[pl.ds(part, rows), s], preferred_element_type=F32)
+            own = vbuf[pl.ds(rows, part), s]
+            mixed[:, s] = jnp.where(giving_all, added / total, own.astype(F32)).astype(jnp.bfloat16)
+            sums = jnp.where(head_lane == c * GROUP + g, top + jnp.log(total), sums)
+        lse_out[...] = sums
+
+    def attend_lo(c):
+        spans = spans_of(c)
+        total_state = jnp.zeros((half, HEAD), F32)
+        found = [scores(qbuf[pl.ds(0, half), s], kbuf[pl.ds(0, rows), s], allowed_lo) for s in spans]
+        for g, s in enumerate(spans):
+            h = c * GROUP + g
+            other = jnp.where(given_rows, lse_in[:, h : h + 1], F32(-1e30))
+            top = jnp.max(found[g], axis=-1, keepdims=True)
+            top = jnp.concatenate([jnp.maximum(top[0:part], other), top[part:]], axis=0)
+            expo = jnp.exp(found[g] - top)
+            total = jnp.sum(expo, axis=-1, keepdims=True)
+            added = jnp.dot(expo.astype(jnp.bfloat16), vbuf[pl.ds(0, rows), s], preferred_element_type=F32)
+            share = jnp.exp(other - top[0:part])
+            first = (added[0:part] + share * vbuf[pl.ds(0, part), s].astype(F32)) / (total[0:part] + share)
+            result = jnp.concatenate([first, added[part:] / total[part:]], axis=0).astype(jnp.bfloat16)
+            obuf[pl.ds(0, half), s] = result
+            total_state = total_state + result.astype(F32) * head_ref[0:1, s]
         return total_state
 
     for load in loads:
         load.wait()
 
-    acc_hi = lax.fori_loop(
-        0, chunks, lambda c, held: held + attend(c, half, half, allowed_hi), jnp.zeros((half, HEAD), F32))
-    acc[pl.ds(half, half), :] = acc_hi
+    def first_phase(c, held):
+        held = held + attend_hi(c)
+
+        @pl.when(sends_on)
+        def _():
+            send_queries(c).wait_recv()
+            attend_next(c)
+            send_mixed(c).start()
+
+        return held
+
+    acc[pl.ds(half, half), :] = lax.fori_loop(0, chunks, first_phase, jnp.zeros((half, HEAD), F32))
+
+    @pl.when(sends_on)
+    def _():
+        send_lse().start()
+
     store_hi = pltpu.make_async_copy(
         obuf.at[pl.ds(half, half)], out_hbm.at[0, pl.ds(half, half)], store_sem.at[0])
     store_hi.start()
 
+    @pl.when(receives)
+    def _():
+        send_lse().wait_recv()
+
     acc_lo = jnp.zeros((half, HEAD), F32)
-    stores = [store_hi]
     for c in range(chunks):
-        @pl.when(tp > 0)
+        @pl.when(receives)
         def _():
-            for copy in exchange(c):
-                copy.wait_recv()
-        acc_lo = acc_lo + attend(c, 0, 0, allowed_lo)
+            send_keys(c).wait_recv()
+            send_mixed(c).wait_recv()
+        acc_lo = acc_lo + attend_lo(c)
+    acc[pl.ds(0, half), :] = acc_lo
     store_lo = pltpu.make_async_copy(
         obuf.at[pl.ds(0, half)], out_hbm.at[0, pl.ds(0, half)], store_sem.at[1])
     store_lo.start()
-    stores.append(store_lo)
-    acc[pl.ds(0, half), :] = acc_lo
+    stores = [store_hi, store_lo]
 
     state = jnp.sum(acc[...].T, axis=0, keepdims=True)
     spot = lax.broadcasted_iota(jnp.int32, (1, rows), 1)
@@ -171,10 +256,10 @@
     square_part = jnp.zeros((1, rows), F32)
     mine = jnp.zeros((1, rows), F32)
     for t in range(n_tp):
-        part = tp_slot[t]
+        held = tp_slot[t]
         arrived = tp_slot[t + 1][5:6] if t + 1 < n_tp else jnp.zeros((1, rows), F32)
-        mean_part = mean_part + part[0:1] + part[2:3] * arrived
-        square_part = square_part + part[1:2] + 2.0 * part[3:4] * arrived + part[4:5] * arrived * arrived
+        mean_part = mean_part + held[0:1] + held[2:3] * arrived
+        square_part = square_part + held[1:2] + 2.0 * held[3:4] * arrived + held[4:5] * arrived * arrived
         mine = jnp.where(tp == t, arrived, mine)
     gae = gae_local + coef * mine
 
@@ -199,9 +284,9 @@
     total_sum = jnp.zeros((1, rows), F32)
     square_sum = jnp.zeros((1, rows), F32)
     for s in range(n_sec):
-        part = sec_slot[s]
-        total_sum = total_sum + part[0:1]
-        square_sum = square_sum + part[1:2]
+        held = sec_slot[s]
+        total_sum = total_sum + held[0:1]
+        square_sum = square_sum + held[1:2]
     number = n_sec * n_tp * rows
     mean = total_sum / number
     spread = square_sum / number - mean * mean
@@ -214,16 +299,22 @@
     for d in range(1, n_sec):
         sec_copy(d).wait_send()
 
-    @pl.when(tp < n_tp - 1)
+    @pl.when(receives)
     def _():
         for c in range(chunks):
-            for copy in exchange(c):
-                copy.wait_send()
+            send_queries(c).wait_send()
+
+    @pl.when(sends_on)
+    def _():
+        for c in range(chunks):
+            send_keys(c).wait_send()
+            send_mixed(c).wait_send()
+        send_lse().wait_send()
 
 
 def local(n_sec, n_tp, queries, key_rows, value_rows, doc_ids, rewards, value_head):
     rows, feat = queries.shape[1:]
-    half = rows // 2
+    part = rows // 4
     chunks = feat // (GROUP * HEAD)
     any_spec = pl.BlockSpec(memory_space=pl.ANY)
     vmem_spec = pl.BlockSpec(memory_space=pltpu.VMEM)
@@ -236,14 +327,18 @@
         out_specs=(any_spec, vmem_spec),
         scratch_shapes=[
             pltpu.VMEM((rows, feat), bf16),
-            pltpu.VMEM((rows + half, feat), bf16),
-            pltpu.VMEM((rows + half, feat), bf16),
+            pltpu.VMEM((rows + part, feat), bf16),
+            pltpu.VMEM((rows + part, feat), bf16),
             pltpu.VMEM((rows, feat), bf16),
+            pltpu.VMEM((part, feat), bf16),
+            pltpu.VMEM((part, feat), bf16),
+            pltpu.VMEM((part, HEAD), F32),
+            pltpu.VMEM((part, HEAD), F32),
             pltpu.VMEM((rows, HEAD), F32),
             pltpu.VMEM((n_tp, 8, rows), F32),
             pltpu.VMEM((n_sec, 8, rows), F32),
             dma((3,)), dma((2,)),
-            dma((chunks,)), dma((chunks,)), dma((chunks,)), dma((chunks,)),
+            dma((chunks,)), dma((chunks,)), dma((chunks,)), dma((chunks,)), dma((chunks,)), dma((chunks,)), dma, dma,
             dma((n_tp,)), dma((n_tp,)), dma((n_sec,)), dma((n_sec,)),
         ],
         compiler_params=pltpu.CompilerParams(collective_id=0, has_side_effects=True),

time: 42.3 us -> 35.6 us (0.84)
  Pallas kernels: 38.6 us -> 31.9 us
    pallas_call x1, Pallas kernels: 38.6 us -> 31.9 us  [local(): pl.pallas_call(functools.partial(kernel, n_sec, n_tp), out_shape=(jax.Sha...]
where the time goes in v2:
time: 35.6 us; the launch traced here: 35.3 us
  Pallas kernels  31.9 us (90%)
  local copies, waits for them, and re-layouts  2.8 us (8%)
  between operations  0.65 us (2%)
    pallas_call x1, Pallas kernels, local(): pl.pallas_call(functools.partial(kernel, n_sec, n_tp), out_shape=(jax.Sha...  31.9 us
    unnamed x4, local copies, waits for them, and re-layouts  2.8 us

profile of v2, /device:TPU:0, one launch (start us, length us, event | category | flops | bytes accessed | tf_op | source)
XLA Modules:
  0.0 35.3 jit_solution(3079747844644768886)
XLA Ops:
  0.6 31.9 %shard_map.77 = (bf16[1,128,4096]{2,1,0:T(8,128)(2,1)}, f32[1,128]{1,0:T(1,128)}) custom-call(bf16[1,128,4096]{2,1,0:T(8,128)(2,1)} %q_hbm.1, bf16[1,128,4096]{2,1,0:T(8,128)(2,1)} %k_hbm.1, bf16[1,128,4096]{2,1,0:T(8,128)(2,1)} %v_hbm.1, s32[1,512]{1,0:T(1,128)} %doc_ref.1, f32[1,128]{1,0:T(1,128)} %rew_ref.1, f32[1,4096]{1,0:T(1,128)} %bitcast.1), custom_call_target="tpu_custom_call" | custom-call | tf_op jit(solution)/shard_map/pallas_call | solution.py:323
  32.5 0.0 copy-start
  32.5 2.3 %copy.10 = bf16[1,128,4096]{2,1,0:T(8,128)(2,1)} copy(bf16[1,128,4096]{2,1,0:T(8,128)(2,1)} %get-tuple-element.4) | data formatting | bytes 2097152
  34.8 0.0 copy-done
  34.8 0.5 %copy.11 = f32[1,128]{1,0:T(1,128)} copy(f32[1,128]{1,0:T(1,128)S(1)} %copy-done) | data formatting | bytes 1024
Async XLA Ops:
  32.5 2.3 %copy-start = (f32[1,128]{1,0:T(1,128)S(1)}, f32[1,128]{1,0:T(1,128)}, u32[]{:S(2)}) copy-start(f32[1,128]{1,0:T(1,128)} %get-tuple-element.5) | copy-start | bytes 1540

commit v3 on v2

--- a/solution.py
+++ b/solution.py
@@ -18,8 +18,8 @@
 F32 = jnp.float32
 
 
-def kernel(n_sec, n_tp, q_hbm, k_hbm, v_hbm, doc_ref, rew_ref, head_ref, out_hbm, adv_ref,
-           qbuf, kbuf, vbuf, obuf, q_in, mixed, lse_out, lse_in, acc, tp_slot, sec_slot,
+def kernel(n_sec, n_tp, q_hbm, k_hbm, v_hbm, doc_hbm, rew_hbm, head_hbm, out_hbm, adv_ref,
+           obuf, doc_ref, rew_ref, head_ref, qbuf, kbuf, vbuf, q_in, mixed, lse_out, lse_in, acc, tp_slot, sec_slot,
            load_sem, store_sem, qsend, qrecv, ksend, krecv, vsend, vrecv, lsend, lrecv,
            tp_send, tp_recv, sec_send, sec_recv):
     rows = qbuf.shape[0]
@@ -31,19 +31,24 @@
     sec = lax.axis_index("sec")
     tp = lax.axis_index("tp")
 
+    barrier = pltpu.get_barrier_semaphore()
+    for d in range(1, n_tp):
+        pl.semaphore_signal(barrier, inc=1, device_id={"tp": lax.rem(tp + d, n_tp)}, device_id_type=MESH)
+    for d in range(1, n_sec):
+        pl.semaphore_signal(barrier, inc=1, device_id={"sec": lax.rem(sec + d, n_sec)}, device_id_type=MESH)
+    small = [
+        pltpu.make_async_copy(doc_hbm, doc_ref, load_sem.at[3]),
+        pltpu.make_async_copy(rew_hbm, rew_ref, load_sem.at[4]),
+        pltpu.make_async_copy(head_hbm, head_ref, load_sem.at[5]),
+    ]
     loads = [
         pltpu.make_async_copy(q_hbm.at[0], qbuf, load_sem.at[0]),
         pltpu.make_async_copy(k_hbm.at[0], kbuf.at[pl.ds(part, rows)], load_sem.at[1]),
         pltpu.make_async_copy(v_hbm.at[0], vbuf.at[pl.ds(part, rows)], load_sem.at[2]),
     ]
-    for load in loads:
+    for load in small + loads:
         load.start()
 
-    barrier = pltpu.get_barrier_semaphore()
-    for d in range(1, n_tp):
-        pl.semaphore_signal(barrier, inc=1, device_id={"tp": lax.rem(tp + d, n_tp)}, device_id_type=MESH)
-    for d in range(1, n_sec):
-        pl.semaphore_signal(barrier, inc=1, device_id={"sec": lax.rem(sec + d, n_sec)}, device_id_type=MESH)
     pl.semaphore_wait(barrier, n_tp + n_sec - 2)
 
     following = {"tp": lax.rem(tp + 1, n_tp)}
@@ -93,6 +98,8 @@
 
     lse_out[...] = jnp.zeros(lse_out.shape, F32)
 
+    for load in small:
+        load.wait()
     start = pl.multiple_of(tp * rows, rows)
     prev = pl.multiple_of(jnp.maximum(tp - 1, 0) * rows, rows)
     after = pl.multiple_of(jnp.minimum(tp + 1, n_tp - 1) * rows, rows)
@@ -189,19 +196,20 @@
         def _():
             send_queries(c).wait_recv()
             attend_next(c)
+
+            @pl.when(c == chunks - 1)
+            def _():
+                send_lse().start()
+
             send_mixed(c).start()
 
         return held
 
     acc[pl.ds(half, half), :] = lax.fori_loop(0, chunks, first_phase, jnp.zeros((half, HEAD), F32))
 
-    @pl.when(sends_on)
-    def _():
-        send_lse().start()
-
-    store_hi = pltpu.make_async_copy(
-        obuf.at[pl.ds(half, half)], out_hbm.at[0, pl.ds(half, half)], store_sem.at[0])
-    store_hi.start()
+    stores = [pltpu.make_async_copy(
+        obuf.at[pl.ds(half, half)], out_hbm.at[pl.ds(half, half)], store_sem.at[chunks])]
+    stores[0].start()
 
     @pl.when(receives)
     def _():
@@ -214,11 +222,11 @@
             send_keys(c).wait_recv()
             send_mixed(c).wait_recv()
         acc_lo = acc_lo + attend_lo(c)
+        store = pltpu.make_async_copy(
+            obuf.at[pl.ds(0, half), columns(c)], out_hbm.at[pl.ds(0, half), columns(c)], store_sem.at[c])
+        store.start()
+        stores.append(store)
     acc[pl.ds(0, half), :] = acc_lo
-    store_lo = pltpu.make_async_copy(
-        obuf.at[pl.ds(0, half)], out_hbm.at[0, pl.ds(0, half)], store_sem.at[1])
-    store_lo.start()
-    stores = [store_hi, store_lo]
 
     state = jnp.sum(acc[...].T, axis=0, keepdims=True)
     spot = lax.broadcasted_iota(jnp.int32, (1, rows), 1)
@@ -312,6 +320,23 @@
         send_lse().wait_send()
 
 
+def finish(attended_hbm, advantages_ref, out_hbm, adv_ref, buf, read_sem, write_sem):
+    pieces = read_sem.shape[0]
+    rows = buf.shape[0] // pieces
+    reads, writes = [], []
+    for i in range(pieces):
+        at = pl.ds(i * rows, rows)
+        reads.append(pltpu.make_async_copy(attended_hbm.at[at], buf.at[at], read_sem.at[i]))
+        writes.append(pltpu.make_async_copy(buf.at[at], out_hbm.at[0, at], write_sem.at[i]))
+        reads[i].start()
+    adv_ref[...] = advantages_ref[...]
+    for i in range(pieces):
+        reads[i].wait()
+        writes[i].start()
+    for write in writes:
+        write.wait()
+
+
 def local(n_sec, n_tp, queries, key_rows, value_rows, doc_ids, rewards, value_head):
     rows, feat = queries.shape[1:]
     part = rows // 4
@@ -320,16 +345,19 @@
     vmem_spec = pl.BlockSpec(memory_space=pltpu.VMEM)
     dma = pltpu.SemaphoreType.DMA
     bf16 = jnp.bfloat16
-    return pl.pallas_call(
+    attended, advantages = pl.pallas_call(
         functools.partial(kernel, n_sec, n_tp),
-        out_shape=(jax.ShapeDtypeStruct((1, rows, feat), bf16), jax.ShapeDtypeStruct((1, rows), F32)),
-        in_specs=[any_spec, any_spec, any_spec, vmem_spec, vmem_spec, vmem_spec],
+        out_shape=(jax.ShapeDtypeStruct((rows, feat), bf16), jax.ShapeDtypeStruct((1, rows), F32)),
+        in_specs=[pl.BlockSpec(memory_space=pltpu.HBM)] * 6,
         out_specs=(any_spec, vmem_spec),
         scratch_shapes=[
             pltpu.VMEM((rows, feat), bf16),
+            pltpu.VMEM(doc_ids.shape, doc_ids.dtype),
+            pltpu.VMEM((1, rows), F32),
+            pltpu.VMEM((1, feat), F32),
+            pltpu.VMEM((rows, feat), bf16),
             pltpu.VMEM((rows + part, feat), bf16),
             pltpu.VMEM((rows + part, feat), bf16),
-            pltpu.VMEM((rows, feat), bf16),
             pltpu.VMEM((part, feat), bf16),
             pltpu.VMEM((part, feat), bf16),
             pltpu.VMEM((part, HEAD), F32),
@@ -337,12 +365,19 @@
             pltpu.VMEM((rows, HEAD), F32),
             pltpu.VMEM((n_tp, 8, rows), F32),
             pltpu.VMEM((n_sec, 8, rows), F32),
-            dma((3,)), dma((2,)),
+            dma((6,)), dma((chunks + 1,)),
             dma((chunks,)), dma((chunks,)), dma((chunks,)), dma((chunks,)), dma((chunks,)), dma((chunks,)), dma, dma,
             dma((n_tp,)), dma((n_tp,)), dma((n_sec,)), dma((n_sec,)),
         ],
         compiler_params=pltpu.CompilerParams(collective_id=0, has_side_effects=True),
     )(queries, key_rows, value_rows, doc_ids, rewards, value_head.reshape(1, feat))
+    return pl.pallas_call(
+        finish,
+        out_shape=(jax.ShapeDtypeStruct((1, rows, feat), bf16), jax.ShapeDtypeStruct((1, rows), F32)),
+        in_specs=[any_spec, vmem_spec],
+        out_specs=(any_spec, vmem_spec),
+        scratch_shapes=[pltpu.VMEM((rows, feat), bf16), dma((4,)), dma((4,))],
+    )(attended, advantages)
 
 
 def solution(mesh):

time: 35.6 us -> 34.3 us (0.963)
  local copies, waits for them, and re-layouts: 2.8 us -> 0 us
  Pallas kernels: 31.9 us -> 33.5 us
    pallas_call x0 -> x1, Pallas kernels: none -> 3.09 us  [local(): pl.pallas_call(finish, out_shape=(jax.ShapeDtypeStruct((1, rows, feat), b...]
    unnamed x4 -> x0, local copies, waits for them, and re-layouts: 2.8 us -> none
    pallas_call x1, Pallas kernels: 31.9 us -> 30.5 us  [local(): pl.pallas_call(functools.partial(kernel, n_sec, n_tp), out_shape=(jax.Sha...]
where the time goes in v3:
time: 34.3 us; the launch traced here: 34.2 us
  Pallas kernels  33.5 us (98%)
  between operations  0.64 us (2%)
    pallas_call x1, Pallas kernels, local(): pl.pallas_call(functools.partial(kernel, n_sec, n_tp), out_shape=(jax.Sha...  30.5 us
    pallas_call x1, Pallas kernels, local(): pl.pallas_call(finish, out_shape=(jax.ShapeDtypeStruct((1, rows, feat), b...  3.09 us

profile of v3, /device:TPU:0, one launch (start us, length us, event | category | flops | bytes accessed | tf_op | source)
XLA Modules:
  0.0 34.2 jit_solution(3907435637639389890)
XLA Ops:
  0.6 30.5 %shard_map.77 = (bf16[128,4096]{1,0:T(8,128)(2,1)}, f32[1,128]{1,0:T(1,128)}) custom-call(bf16[1,128,4096]{2,1,0:T(8,128)(2,1)} %q_hbm.1, bf16[1,128,4096]{2,1,0:T(8,128)(2,1)} %k_hbm.1, bf16[1,128,4096]{2,1,0:T(8,128)(2,1)} %v_hbm.1, s32[1,512]{1,0:T(1,128)} %doc_hbm.1, f32[1,128]{1,0:T(1,128)} %rew_hbm.1, f32[1,4096]{1,0:T(1,128)} %bitcast.1), custom_call_target="tpu_custom_call" | custom-call | tf_op jit(solution)/shard_map/pallas_call | solution.py:348
  31.1 3.1 %shard_map.78 = (bf16[1,128,4096]{2,1,0:T(8,128)(2,1)}, f32[1,128]{1,0:T(1,128)}) custom-call(bf16[128,4096]{1,0:T(8,128)(2,1)} %get-tuple-element.4.attended_hbm, f32[1,128]{1,0:T(1,128)} %get-tuple-element.5.advantages_ref), custom_call_target="tpu_custom_call" | custom-call | tf_op jit(solution)/shard_map/pallas_call | solution.py:374

commit v4 on v3

--- a/solution.py
+++ b/solution.py
@@ -18,9 +18,9 @@
 F32 = jnp.float32
 
 
-def kernel(n_sec, n_tp, q_hbm, k_hbm, v_hbm, doc_hbm, rew_hbm, head_hbm, out_hbm, adv_ref,
-           obuf, doc_ref, rew_ref, head_ref, qbuf, kbuf, vbuf, q_in, mixed, lse_out, lse_in, acc, tp_slot, sec_slot,
-           load_sem, store_sem, qsend, qrecv, ksend, krecv, vsend, vrecv, lsend, lrecv,
+def kernel(n_sec, n_tp, q_hbm, k_hbm, v_hbm, doc_hbm, rew_hbm, head_hbm, obuf, adv_ref,
+           doc_ref, rew_ref, head_ref, qbuf, kbuf, vbuf, q_in, mixed, lse_out, lse_in, acc, tp_slot, sec_slot,
+           load_sem, qsend, qrecv, ksend, krecv, vsend, vrecv, lsend, lrecv,
            tp_send, tp_recv, sec_send, sec_recv):
     rows = qbuf.shape[0]
     feat = qbuf.shape[1]
@@ -207,10 +207,6 @@
 
     acc[pl.ds(half, half), :] = lax.fori_loop(0, chunks, first_phase, jnp.zeros((half, HEAD), F32))
 
-    stores = [pltpu.make_async_copy(
-        obuf.at[pl.ds(half, half)], out_hbm.at[pl.ds(half, half)], store_sem.at[chunks])]
-    stores[0].start()
-
     @pl.when(receives)
     def _():
         send_lse().wait_recv()
@@ -222,10 +218,6 @@
             send_keys(c).wait_recv()
             send_mixed(c).wait_recv()
         acc_lo = acc_lo + attend_lo(c)
-        store = pltpu.make_async_copy(
-            obuf.at[pl.ds(0, half), columns(c)], out_hbm.at[pl.ds(0, half), columns(c)], store_sem.at[c])
-        store.start()
-        stores.append(store)
     acc[pl.ds(0, half), :] = acc_lo
 
     state = jnp.sum(acc[...].T, axis=0, keepdims=True)
@@ -300,8 +292,6 @@
     spread = square_sum / number - mean * mean
     adv_ref[...] = (gae - mean) / jnp.sqrt(spread + epsilon)
 
-    for store in stores:
-        store.wait()
     for d in range(1, n_tp):
         tp_copy(d).wait_send()
     for d in range(1, n_sec):
@@ -320,21 +310,11 @@
         send_lse().wait_send()
 
 
-def finish(attended_hbm, advantages_ref, out_hbm, adv_ref, buf, read_sem, write_sem):
-    pieces = read_sem.shape[0]
-    rows = buf.shape[0] // pieces
-    reads, writes = [], []
-    for i in range(pieces):
-        at = pl.ds(i * rows, rows)
-        reads.append(pltpu.make_async_copy(attended_hbm.at[at], buf.at[at], read_sem.at[i]))
-        writes.append(pltpu.make_async_copy(buf.at[at], out_hbm.at[0, at], write_sem.at[i]))
-        reads[i].start()
+def finish(attended_ref, advantages_ref, out_hbm, adv_ref, sem):
+    copy = pltpu.make_async_copy(attended_ref, out_hbm.at[0], sem)
+    copy.start()
     adv_ref[...] = advantages_ref[...]
-    for i in range(pieces):
-        reads[i].wait()
-        writes[i].start()
-    for write in writes:
-        write.wait()
+    copy.wait()
 
 
 def local(n_sec, n_tp, queries, key_rows, value_rows, doc_ids, rewards, value_head):
@@ -345,13 +325,14 @@
     vmem_spec = pl.BlockSpec(memory_space=pltpu.VMEM)
     dma = pltpu.SemaphoreType.DMA
     bf16 = jnp.bfloat16
+    held = [pltpu.with_memory_space_constraint(x, pltpu.HBM) for x in (
+        queries, key_rows, value_rows, doc_ids, rewards, value_head.reshape(1, feat))]
     attended, advantages = pl.pallas_call(
         functools.partial(kernel, n_sec, n_tp),
         out_shape=(jax.ShapeDtypeStruct((rows, feat), bf16), jax.ShapeDtypeStruct((1, rows), F32)),
         in_specs=[pl.BlockSpec(memory_space=pltpu.HBM)] * 6,
-        out_specs=(any_spec, vmem_spec),
+        out_specs=(vmem_spec, vmem_spec),
         scratch_shapes=[
-            pltpu.VMEM((rows, feat), bf16),
             pltpu.VMEM(doc_ids.shape, doc_ids.dtype),
             pltpu.VMEM((1, rows), F32),
             pltpu.VMEM((1, feat), F32),
@@ -365,18 +346,19 @@
             pltpu.VMEM((rows, HEAD), F32),
             pltpu.VMEM((n_tp, 8, rows), F32),
             pltpu.VMEM((n_sec, 8, rows), F32),
-            dma((6,)), dma((chunks + 1,)),
+            dma((6,)),
             dma((chunks,)), dma((chunks,)), dma((chunks,)), dma((chunks,)), dma((chunks,)), dma((chunks,)), dma, dma,
             dma((n_tp,)), dma((n_tp,)), dma((n_sec,)), dma((n_sec,)),
         ],
-        compiler_params=pltpu.CompilerParams(collective_id=0, has_side_effects=True),
-    )(queries, key_rows, value_rows, doc_ids, rewards, value_head.reshape(1, feat))
+        compiler_params=pltpu.CompilerParams(collective_id=0, has_side_effects=True, vmem_limit_bytes=24 << 20),
+    )(*held)
     return pl.pallas_call(
         finish,
         out_shape=(jax.ShapeDtypeStruct((1, rows, feat), bf16), jax.ShapeDtypeStruct((1, rows), F32)),
-        in_specs=[any_spec, vmem_spec],
+        in_specs=[vmem_spec, vmem_spec],
         out_specs=(any_spec, vmem_spec),
-        scratch_shapes=[pltpu.VMEM((rows, feat), bf16), dma((4,)), dma((4,))],
+        scratch_shapes=[dma],
+        compiler_params=pltpu.CompilerParams(vmem_limit_bytes=24 << 20),
     )(attended, advantages)
 
 

time: 34.3 us -> 32.2 us (0.939)
  Pallas kernels: 33.5 us -> 31.4 us
    pallas_call x1, Pallas kernels: 3.09 us -> 1.49 us  [local(): pl.pallas_call(finish, out_shape=(jax.ShapeDtypeStruct((1, rows, feat), b...]
    pallas_call x1, Pallas kernels: 30.5 us -> 29.9 us  [local(): pl.pallas_call(functools.partial(kernel, n_sec, n_tp), out_shape=(jax.Sha...]
where the time goes in v4:
time: 32.2 us; the launch traced here: 32 us
  Pallas kernels  31.4 us (98%)
  between operations  0.64 us (2%)
    pallas_call x1, Pallas kernels, local(): pl.pallas_call(functools.partial(kernel, n_sec, n_tp), out_shape=(jax.Sha...  29.9 us
    pallas_call x1, Pallas kernels, local(): pl.pallas_call(finish, out_shape=(jax.ShapeDtypeStruct((1, rows, feat), b...  1.49 us

profile of v4, /device:TPU:0, one launch (start us, length us, event | category | flops | bytes accessed | tf_op | source)
XLA Modules:
  0.0 32.0 jit_solution(13363105772222712354)
XLA Ops:
  0.6 29.9 %shard_map.77 = (bf16[128,4096]{1,0:T(8,128)(2,1)S(1)}, f32[1,128]{1,0:T(1,128)S(1)}) custom-call(bf16[1,128,4096]{2,1,0:T(8,128)(2,1)} %q_hbm.1, bf16[1,128,4096]{2,1,0:T(8,128)(2,1)} %k_hbm.1, bf16[1,128,4096]{2,1,0:T(8,128)(2,1)} %v_hbm.1, s32[1,512]{1,0:T(1,128)} %doc_hbm.1, f32[1,128]{1,0:T(1,128)} %rew_hbm.1, f32[1,4096]{1,0:T(1,128)} %bitcast.1), custom_call_target="tpu_custom_call" | custom-call | tf_op jit(solution)/shard_map/pallas_call | solution.py:330
  30.5 1.5 %shard_map.78 = (bf16[1,128,4096]{2,1,0:T(8,128)(2,1)}, f32[1,128]{1,0:T(1,128)}) custom-call(bf16[128,4096]{1,0:T(8,128)(2,1)S(1)} %get-tuple-element.4.attended_ref, f32[1,128]{1,0:T(1,128)S(1)} %get-tuple-element.5.advantages_ref), custom_call_target="tpu_custom_call" | custom-call | tf_op jit(solution)/shard_map/pallas_call | solution.py:355

commit v5 on v4

--- a/solution.py
+++ b/solution.py
@@ -9,7 +9,7 @@
 from jax.sharding import PartitionSpec as P
 
 HEAD = 128
-GROUP = 8
+GROUP = 4
 
 gae_decay = 0.95
 epsilon = 1e-05
@@ -311,10 +311,16 @@
 
 
 def finish(attended_ref, advantages_ref, out_hbm, adv_ref, sem):
-    copy = pltpu.make_async_copy(attended_ref, out_hbm.at[0], sem)
-    copy.start()
+    pieces = sem.shape[0]
+    rows = attended_ref.shape[0] // pieces
+    writes = []
+    for i in range(pieces):
+        at = pl.ds(i * rows, rows)
+        writes.append(pltpu.make_async_copy(attended_ref.at[at], out_hbm.at[0, at], sem.at[i]))
+        writes[i].start()
     adv_ref[...] = advantages_ref[...]
-    copy.wait()
+    for write in writes:
+        write.wait()
 
 
 def local(n_sec, n_tp, queries, key_rows, value_rows, doc_ids, rewards, value_head):
@@ -357,7 +363,7 @@
         out_shape=(jax.ShapeDtypeStruct((1, rows, feat), bf16), jax.ShapeDtypeStruct((1, rows), F32)),
         in_specs=[vmem_spec, vmem_spec],
         out_specs=(any_spec, vmem_spec),
-        scratch_shapes=[dma],
+        scratch_shapes=[dma((4,))],
         compiler_params=pltpu.CompilerParams(vmem_limit_bytes=24 << 20),
     )(attended, advantages)
 

time: 32.2 us -> 32.3 us (level)
  no operation moved by 1% of the time
where the time goes in v5:
time: 32.3 us; the launch traced here: 32.2 us
  Pallas kernels  31.5 us (98%)
  between operations  0.64 us (2%)
    pallas_call x1, Pallas kernels, local(): pl.pallas_call(functools.partial(kernel, n_sec, n_tp), out_shape=(jax.Sha...  30 us
    pallas_call x1, Pallas kernels, local(): pl.pallas_call(finish, out_shape=(jax.ShapeDtypeStruct((1, rows, feat), b...  1.51 us

profile of v5, /device:TPU:0, one launch (start us, length us, event | category | flops | bytes accessed | tf_op | source)
XLA Modules:
  0.0 32.2 jit_solution(9466822837556692817)
XLA Ops:
  0.6 30.0 %shard_map.77 = (bf16[128,4096]{1,0:T(8,128)(2,1)S(1)}, f32[1,128]{1,0:T(1,128)S(1)}) custom-call(bf16[1,128,4096]{2,1,0:T(8,128)(2,1)} %q_hbm.1, bf16[1,128,4096]{2,1,0:T(8,128)(2,1)} %k_hbm.1, bf16[1,128,4096]{2,1,0:T(8,128)(2,1)} %v_hbm.1, s32[1,512]{1,0:T(1,128)} %doc_hbm.1, f32[1,128]{1,0:T(1,128)} %rew_hbm.1, f32[1,4096]{1,0:T(1,128)} %bitcast.1), custom_call_target="tpu_custom_call" | custom-call | tf_op jit(solution)/shard_map/pallas_call | solution.py:336
  30.7 1.5 %shard_map.78 = (bf16[1,128,4096]{2,1,0:T(8,128)(2,1)}, f32[1,128]{1,0:T(1,128)}) custom-call(bf16[128,4096]{1,0:T(8,128)(2,1)S(1)} %get-tuple-element.4.attended_ref, f32[1,128]{1,0:T(1,128)S(1)} %get-tuple-element.5.advantages_ref), custom_call_target="tpu_custom_call" | custom-call | tf_op jit(solution)/shard_map/pallas_call | solution.py:361
